TPU v7x, 32 devices: a whole 2x2x4 slice. The times are simulated.
32 devices in a mesh: space: 8 (over z, y), chan: 2 (over core), filt: 2 (over x).
Axes of the slice: x: 2, y: 2, z: 4, core: 2. Of those that a mesh axis runs over, the one named last changes fastest.
Arguments:
- activation: bfloat16 [8, 512, 512], P('space', ('chan', 'filt')), may hold values from -6 to 6
- kernel: bfloat16 [3, 3, 3, 512, 512], P(None, None, None, 'filt', 'chan'), may hold values from -0.0546875 to 0.0546875
- out_grad: bfloat16 [8, 512, 512], P('space', 'filt', 'chan'), may hold values from -6 to 6
Outputs:
- output: bfloat16 [8, 512, 512], P('space', 'filt', 'chan')
- input_grad: bfloat16 [8, 512, 512], P('space', ('chan', 'filt'))
- kernel_grad: float32 [3, 3, 3, 512, 512], P(None, None, None, 'filt', 'chan')
All inputs are finite; a program needn't handle non-finite values.
Results may differ from a plain program's by a relative error of at most 0.001.
Values may be sent and summed in bfloat16 or wider, within the bound.
A program may use at most 128 MiB of HBM per device.

v0:
```python
import jax
import jax.numpy as jnp
from jax import lax
from jax.sharding import PartitionSpec as P

W = 16


def padded(x, sides, width):
    for axis, dim in sides:
        size, length = (lax.axis_size(axis), x.shape[dim])
        up = [(i, (i + 1) % size) for i in range(size - 1)]
        down = [(j, i) for i, j in up]
        last = lax.slice_in_dim(x, length - width, length, axis=dim)
        first = lax.slice_in_dim(x, 0, width, axis=dim)
        before = lax.ppermute(last, axis, up)
        after = lax.ppermute(first, axis, down)
        x = jnp.concatenate([before, x, after], axis=dim)
    return x


def plane_window(widened, plane, row_step, col_step, masks):
    begin = row_step * W + col_step
    return widened[:, :, begin : begin + plane] * masks[col_step]


def body(activation, kernel, out_grad):
    depth = activation.shape[0]
    plane = activation.shape[2]
    panels = lax.all_gather(activation, "filt", axis=1, tiled=True)
    rimmed = padded(panels, (("space", 0),), 1)
    grad_full = lax.all_gather(out_grad, "chan", axis=2, tiled=True)
    grad_rimmed = padded(grad_full, (("space", 0),), 1)
    column = lax.iota(jnp.int32, plane) % W
    masks = [
        ((column + step - 1 >= 0) & (column + step - 1 < W)).astype(jnp.bfloat16)
        for step in range(3)
    ]
    chan_local = rimmed.shape[1]
    filt_local = grad_rimmed.shape[1]
    wide_input = jnp.pad(rimmed, ((0, 0), (0, 0), (W + 1, W + 1)))
    wide_grad = jnp.pad(grad_rimmed, ((0, 0), (0, 0), (W + 1, W + 1)))
    forward = jnp.zeros((depth, filt_local, plane), jnp.float32)
    backward = jnp.zeros((depth, chan_local, plane), jnp.float32)
    taps = []
    for a in range(3):
        input_slab = wide_input[a : a + depth]
        grad_slab = wide_grad[2 - a : 2 - a + depth]
        for b in range(3):
            window = jnp.concatenate(
                [plane_window(input_slab, plane, b, c, masks) for c in range(3)], axis=1
            )
            grad_window = jnp.concatenate(
                [plane_window(grad_slab, plane, 2 - b, 2 - c, masks) for c in range(3)], axis=1
            )
            weights = kernel[a, b]
            forward_weights = weights.transpose(1, 0, 2).reshape(filt_local, 3 * chan_local)
            backward_weights = weights.reshape(3 * filt_local, chan_local)
            forward = forward + jnp.einsum(
                "fk,zkp->zfp", forward_weights, window, preferred_element_type=jnp.float32
            )
            backward = backward + jnp.einsum(
                "fk,zfp->zkp", backward_weights, grad_window, preferred_element_type=jnp.float32
            )
            joined = jnp.einsum(
                "zfp,zkp->fk", grad_full, window, preferred_element_type=jnp.float32
            )
            taps.append(joined.reshape(filt_local, 3, chan_local).transpose(1, 0, 2))
    output = lax.psum_scatter(forward, "chan", scatter_dimension=2, tiled=True).astype(jnp.bfloat16)
    input_grad = lax.psum_scatter(backward, "filt", scatter_dimension=1, tiled=True).astype(
        jnp.bfloat16
    )
    local_grad = jnp.stack(taps).reshape(3, 3, 3, filt_local, chan_local)
    total = lax.psum(local_grad, "space")
    cells = depth * lax.axis_size("space") * plane
    kernel_grad = total / jnp.sqrt(jnp.float32(cells))
    return (output, input_grad, kernel_grad)


def solution(mesh):
    placed = (
        P("space", ("chan", "filt"), None),
        P(None, None, None, "filt", "chan"),
        P("space", "filt", "chan"),
    )
    return jax.shard_map(
        body,
        mesh=mesh,
        in_specs=placed,
        out_specs=(
            P("space", "filt", "chan"),
            P("space", ("chan", "filt"), None),
            P(None, None, None, "filt", "chan"),
        ),
        check_vma=False,
    )
```

profile of v0, /device:TPU:0, one launch (start us, length us, event | category | flops | bytes accessed | tf_op | source)
XLA Modules:
  0.0 349.9 jit_solution(17022431209506651574)
XLA Ops:
  8.0 7.4 %all_gather.6 = bf16[1,256,512]{2,1,0:T(8,128)(2,1)S(1)} all-gather(bf16[1,128,512]{2,1,0:T(8,128)(2,1)} %param.3), channel_id=1, replica_groups=mesh['space'=8,'chan'=2,'filt'=2] {'filt'}, dimensions={1}, use_global_device_ids=true | all-gather | bytes 393216 | tf_op jit(solution)/shard_map/all_gather | solution.py:30
  15.4 1.3 collective-permute-start.1
  16.7 5.3 %collective-permute-start = (bf16[1,256,512]{2,1,0:T(8,128)(2,1)S(1)}, bf16[1,256,512]{2,1,0:T(8,128)(2,1)}, u32[]{:S(2)}, u32[]{:S(2)}) collective-permute-start(bf16[1,256,512]{2,1,0:T(8,128)(2,1)S(1)} %all_gather.6), channel_id=1, source_target_pairs={{0,4},{4,8},{8,12},{12,16},{16,20},{20,24},{24,28},{1,5},{5,9},{9,... | collective-permute-start | bytes 786440 | tf_op jit(solution)/shard_map/ppermute | solution.py:16
  22.0 2.3 all_gather.7
  24.2 4.5 %collective-permute-start.2 = (bf16[1,256,512]{2,1,0:T(8,128)(2,1)S(1)}, bf16[1,256,512]{2,1,0:T(8,128)(2,1)}, u32[]{:S(2)}, u32[]{:S(2)}) collective-permute-start(bf16[1,256,512]{2,1,0:T(8,128)(2,1)S(1)} %all_gather.7), channel_id=1, source_target_pairs={{0,4},{4,8},{8,12},{12,16},{16,20},{20,24},{24,28},{1,5},{5,9},{9,... | collective-permute-start | bytes 786440 | tf_op jit(solution)/shard_map/ppermute | solution.py:16
  28.8 1.3 collective-permute-start.3
  30.1 3.2 fusion.87
  33.3 2.3 copy.42
  35.6 1.9 copy.43
  44.1 1.5 select_maximum_fusion.2
  46.3 1.6 select_maximum_fusion
  48.0 1.9 slice_multiply_fusion
  49.8 2.8 slice_multiply_fusion.26
  53.0 4.0 %slice_multiply_fusion.2 = (bf16[1,256,512]{2,1,0:T(8,128)(2,1)}, bf16[1,256,512]{2,1,0:T(8,128)(2,1)}, bf16[1,256,512]{2,1,0:T(8,128)(2,1)}, bf16[1,256,512]{2,...) fusion(bf16[3,256,546]{2,1,0:T(8,128)(2,1)S(1)} %select_maximum, ...), kind=kLoop, calls=%fused_computation.112 | loop fusion | flops 2228224 | bytes 8914944 | tf_op jit(solution)/shard_map/mul | solution.py:24
  64.6 1.8 broadcast_multiply_fusion.3
  66.4 1.3 pad_maximum_fusion.6
  70.1 1.6 fusion.13
  88.0 1.3 fusion.5
  89.3 1.3 fusion.4
  90.5 1.3 fusion.3
  91.8 1.3 fusion.2
  94.4 8.1 %copy.39 = f32[3,3,3,256,256]{4,3,2,1,0:T(8,128)} copy(f32[3,3,3,256,256]{3,4,2,1,0:T(8,128)} %bitcast.227) | data formatting | bytes 14155776 | tf_op jit(solution)/shard_map/reshape | solution.py:73
  106.0 229.8 %all-reduce.4.cloned.1.call-done = f32[3,3,3,256,256]{4,3,2,1,0:T(8,128)} async-done(((f32[3,3,3,256,256]{4,3,2,1,0:T(8,128)}), f32[3,3,3,256,256]{4,3,2,1,0:T(8,128)}) %all-reduce.4.cloned.1.call-update) | async-done | bytes 7077904 | tf_op jit(solution)/shard_map/psum | solution.py:74
  335.8 6.7 %broadcast_multiply_fusion = f32[3,3,3,256,256]{4,3,2,1,0:T(8,128)} fusion(f32[3,3,3,256,256]{4,3,2,1,0:T(8,128)} %all-reduce.4.cloned.1.call-done), kind=kLoop, calls=%fused_computation | loop fusion | flops 1769472 | bytes 14155776 | tf_op jit(solution)/shard_map/div | solution.py:76
  (173 shorter events, 38.4 us)
Async XLA Ops:
  8.0 94.5 %reduce-scatter.3.cloned.1.call-start = ((), (), s32[]{:S(2)}) async-start(), calls=%async_computation.2 | async-start | bytes 786432 | tf_op jit(solution)/shard_map/reduce_scatter | solution.py:69
  15.4 28.7 %collective-permute-start.1 = (bf16[1,256,512]{2,1,0:T(8,128)(2,1)S(1)}, bf16[1,256,512]{2,1,0:T(8,128)(2,1)}, u32[]{:S(2)}, u32[]{:S(2)}) collective-permute-start(bf16[1,256,512]{2,1,0:T(8,128)(2,1)S(1)} %all_gather.6), channel_id=1, source_target_pairs={{4,0},{8,4},{12,8},{16,12},{20,16},{24,20},{28,24},{5,1},{9,5},{13... | collective-permute-start | bytes 786440 | tf_op jit(solution)/shard_map/ppermute | solution.py:17
  16.7 27.4 %collective-permute-start = (bf16[1,256,512]{2,1,0:T(8,128)(2,1)S(1)}, bf16[1,256,512]{2,1,0:T(8,128)(2,1)}, u32[]{:S(2)}, u32[]{:S(2)}) collective-permute-start(bf16[1,256,512]{2,1,0:T(8,128)(2,1)S(1)} %all_gather.6), channel_id=1, source_target_pairs={{0,4},{4,8},{8,12},{12,16},{16,20},{20,24},{24,28},{1,5},{5,9},{9,... | collective-permute-start | bytes 786440 | tf_op jit(solution)/shard_map/ppermute | solution.py:16
  24.2 22.1 %collective-permute-start.2 = (bf16[1,256,512]{2,1,0:T(8,128)(2,1)S(1)}, bf16[1,256,512]{2,1,0:T(8,128)(2,1)}, u32[]{:S(2)}, u32[]{:S(2)}) collective-permute-start(bf16[1,256,512]{2,1,0:T(8,128)(2,1)S(1)} %all_gather.7), channel_id=1, source_target_pairs={{0,4},{4,8},{8,12},{12,16},{16,20},{20,24},{24,28},{1,5},{5,9},{9,... | collective-permute-start | bytes 786440 | tf_op jit(solution)/shard_map/ppermute | solution.py:16
  28.8 17.6 %collective-permute-start.3 = (bf16[1,256,512]{2,1,0:T(8,128)(2,1)S(1)}, bf16[1,256,512]{2,1,0:T(8,128)(2,1)}, u32[]{:S(2)}, u32[]{:S(2)}) collective-permute-start(bf16[1,256,512]{2,1,0:T(8,128)(2,1)S(1)} %all_gather.7), channel_id=1, source_target_pairs={{4,0},{8,4},{12,8},{16,12},{20,16},{24,20},{28,24},{5,1},{9,5},{13... | collective-permute-start | bytes 786440 | tf_op jit(solution)/shard_map/ppermute | solution.py:17
  33.3 6.1 %copy-start.15 = (bf16[1,1,3,256,256]{4,3,2,1,0:T(8,128)(2,1)}, bf16[1,1,3,256,256]{4,3,2,1,0:T(8,128)(2,1)S(1)}, u32[]{:S(2)}) copy-start(bf16[1,1,3,256,256]{4,3,2,1,0:T(8,128)(2,1)S(1)} %get-tuple-element.17) | copy-start | bytes 1179652
  33.3 6.1 %copy-start.17 = (bf16[1,1,3,256,256]{4,3,2,1,0:T(8,128)(2,1)}, bf16[1,1,3,256,256]{4,3,2,1,0:T(8,128)(2,1)S(1)}, u32[]{:S(2)}) copy-start(bf16[1,1,3,256,256]{4,3,2,1,0:T(8,128)(2,1)S(1)} %get-tuple-element.18) | copy-start | bytes 1179652
  33.3 6.1 %copy-start.13 = (bf16[1,1,3,256,256]{4,3,2,1,0:T(8,128)(2,1)}, bf16[1,1,3,256,256]{4,3,2,1,0:T(8,128)(2,1)S(1)}, u32[]{:S(2)}) copy-start(bf16[1,1,3,256,256]{4,3,2,1,0:T(8,128)(2,1)S(1)} %get-tuple-element.16) | copy-start | bytes 1179652
  33.3 7.0 %copy-start.11 = (bf16[1,1,3,256,256]{4,3,2,1,0:T(8,128)(2,1)}, bf16[1,1,3,256,256]{4,3,2,1,0:T(8,128)(2,1)S(1)}, u32[]{:S(2)}) copy-start(bf16[1,1,3,256,256]{4,3,2,1,0:T(8,128)(2,1)S(1)} %get-tuple-element.15) | copy-start | bytes 1179652
  33.3 7.9 %copy-start.9 = (bf16[1,1,3,256,256]{4,3,2,1,0:T(8,128)(2,1)}, bf16[1,1,3,256,256]{4,3,2,1,0:T(8,128)(2,1)S(1)}, u32[]{:S(2)}) copy-start(bf16[1,1,3,256,256]{4,3,2,1,0:T(8,128)(2,1)S(1)} %get-tuple-element.14) | copy-start | bytes 1179652
  33.3 8.8 %copy-start.7 = (bf16[1,1,3,256,256]{4,3,2,1,0:T(8,128)(2,1)}, bf16[1,1,3,256,256]{4,3,2,1,0:T(8,128)(2,1)S(1)}, u32[]{:S(2)}) copy-start(bf16[1,1,3,256,256]{4,3,2,1,0:T(8,128)(2,1)S(1)} %get-tuple-element.13) | copy-start | bytes 1179652
  33.3 9.8 %copy-start.5 = (bf16[1,1,3,256,256]{4,3,2,1,0:T(8,128)(2,1)}, bf16[1,1,3,256,256]{4,3,2,1,0:T(8,128)(2,1)S(1)}, u32[]{:S(2)}) copy-start(bf16[1,1,3,256,256]{4,3,2,1,0:T(8,128)(2,1)S(1)} %get-tuple-element.12) | copy-start | bytes 1179652
  46.3 21.7 %copy-start.21 = (bf16[1,256,512]{2,1,0:T(8,128)(2,1)}, bf16[1,256,512]{2,1,0:T(8,128)(2,1)S(1)}, u32[]{:S(2)}) copy-start(bf16[1,256,512]{2,1,0:T(8,128)(2,1)S(1)} %get-tuple-element.60) | copy-start | bytes 786436
  49.8 2.8 copy-start.35
  52.6 15.5 %copy-start.23 = (bf16[1,256,512]{2,1,0:T(8,128)(2,1)}, bf16[1,256,512]{2,1,0:T(8,128)(2,1)S(1)}, u32[]{:S(2)}) copy-start(bf16[1,256,512]{2,1,0:T(8,128)(2,1)S(1)} %get-tuple-element.45) | copy-start | bytes 786436
  52.6 15.5 %copy-start.25 = (bf16[1,256,512]{2,1,0:T(8,128)(2,1)}, bf16[1,256,512]{2,1,0:T(8,128)(2,1)S(1)}, u32[]{:S(2)}) copy-start(bf16[1,256,512]{2,1,0:T(8,128)(2,1)S(1)} %get-tuple-element.80) | copy-start | bytes 786436
  69.9 34.4 %reduce-scatter.5.cloned.1.call-start = ((), (), s32[]{:S(2)}) async-start(), calls=%async_computation.3 | async-start | bytes 786432 | tf_op jit(solution)/shard_map/reduce_scatter | solution.py:70
  70.1 1.7 copy-start.19
  70.1 1.7 copy-start.46
  84.1 251.7 %all-reduce.4.cloned.1.call-start = ((), (), s32[]{:S(2)}) async-start(), calls=%async_computation.4 | async-start | bytes 14155776 | tf_op jit(solution)/shard_map/psum | solution.py:74
  85.4 2.6 copy-start.2
  86.7 2.6 copy-start.1
  88.0 2.6 copy-start.4
  89.3 2.6 copy-start.3
  (43 other events, 48.9 us)
Sparse Core Ops, SparseCore 0:
  70.0 9.3 reduce-scatter.2
  84.2 16.0 reduce-scatter.4
Sparse Core Ops, SparseCore 1:
  102.6 233.1 all-reduce.3
where the time goes:
time: 351 us; the launch traced here: 350 us
  waiting for transfers between devices  230 us (66%)
  local copies, waits for them, and re-layouts  33.5 us (10%)
  other arithmetic  26.6 us (8%)
  matrix products  21.7 us (6%)
  between operations  16 us (5%)
  starting transfers between devices  12.7 us (4%)
  blocking collectives  9.65 us (3%)
    psum x1, waiting for transfers between devices, body(): total = lax.psum(local_grad, 'space')  230 us
    unnamed x131, local copies, waits for them, and re-layouts  22.2 us
    dot_general x9, matrix products, body(): jnp.einsum('zfp,zkp->fk', grad_full, window, preferred_element_type=jnp.f...  11.5 us
    mul x5, other arithmetic, plane_window(): return widened[:, :, begin:begin + plane] * masks[col_step]  11.1 us
    ppermute x2, starting transfers between devices, padded(): before = lax.ppermute(last, axis, up)  9.8 us
    reshape x1, local copies, waits for them, and re-layouts, body(): local_grad = jnp.stack(taps).reshape(3, 3, 3, filt_local, chan_local)  8.09 us
    all_gather x1, blocking collectives, body(): panels = lax.all_gather(activation, 'filt', axis=1, tiled=True)  7.36 us
  transfers between devices with their start and end apart: 7, of which 1 were waited for; matrix products, arithmetic and copies ran while one was open for 13% of the time, Pallas kernels for 0%

commit v1 on v0

--- a/solution.py
+++ b/solution.py
@@ -71,7 +71,8 @@
         jnp.bfloat16
     )
     local_grad = jnp.stack(taps).reshape(3, 3, 3, filt_local, chan_local)
-    total = lax.psum(local_grad, "space")
+    shards = lax.all_gather(local_grad, "space", axis=0, tiled=False)
+    total = shards.sum(axis=0)
     cells = depth * lax.axis_size("space") * plane
     kernel_grad = total / jnp.sqrt(jnp.float32(cells))
     return (output, input_grad, kernel_grad)

time: 351 us -> 1220 us (3.48)
  waiting for transfers between devices: 230 us -> 1070 us
  other arithmetic: 26.6 us -> 47.1 us
  local copies, waits for them, and re-layouts: 33.5 us -> 46.5 us
    all_gather x0 -> x1, waiting for transfers between devices: none -> 1070 us  [body(): shards = lax.all_gather(local_grad, 'space', axis=0, tiled=False)]
    psum x1 -> x0, waiting for transfers between devices: 230 us -> none  [body(): total = lax.psum(local_grad, 'space')]
    reduce_sum x0 -> x1, other arithmetic: none -> 21.5 us  [body(): total = shards.sum(axis=0)]
    unnamed x131 -> x105, local copies, waits for them, and re-layouts: 22.2 us -> 35.3 us
  transfers between devices with their start and end apart: 7 -> 7, of which waited for: 1 -> 1; matrix products, arithmetic and copies ran while one was open for 13% -> 4% of each run, Pallas kernels for 0% -> 0%
where the time goes in v1:
time: 1220 us
  waiting for transfers between devices  1070 us (88%)
  other arithmetic  47.1 us (4%)
  local copies, waits for them, and re-layouts  46.5 us (4%)
  matrix products  20.4 us (2%)
  between operations  16 us (1%)
  starting transfers between devices  12.7 us (1%)
    all_gather x1, waiting for transfers between devices, body(): shards = lax.all_gather(local_grad, 'space', axis=0, tiled=False)  1070 us
    unnamed x105, local copies, waits for them, and re-layouts  35.3 us
  transfers between devices with their start and end apart: 7, of which 1 were waited for; matrix products, arithmetic and copies ran while one was open for 4% of the time, Pallas kernels for 0%

profile of v1, /device:TPU:0, one launch (start us, length us, event | category | flops | bytes accessed | tf_op | source)
XLA Modules:
  0.0 1220.9 jit_solution(5308959309423740087)
XLA Ops:
  8.0 7.4 all_gather.9
  15.4 1.3 collective-permute-start.1
  16.7 5.3 collective-permute-start
  22.0 2.3 all_gather.10
  24.3 1.3 collective-permute-start.3
  25.5 4.6 collective-permute-start.2
  30.1 3.1 fusion.87
  39.7 1.9 copy.64
  41.6 1.9 copy.63
  43.6 1.5 select_maximum_fusion
  45.7 1.5 select_maximum_fusion.2
  47.2 2.0 slice_multiply_fusion.24
  49.3 3.0 slice_multiply_fusion.2
  55.5 2.7 slice_multiply_fusion.26
  72.0 1.3 pad_maximum_fusion.6
  82.8 1.3 fusion.5
  84.1 1.3 fusion.4
  85.4 1.3 fusion.3
  89.2 8.1 copy.57
  100.9 1068.4 %all-gather.2.cloned.1.call-done = f32[8,3,3,3,256,256]{5,4,3,2,1,0:T(8,128)} async-done(((f32[1,3,3,3,256,256]{5,4,3,2,1,0:T(8,128)}), f32[8,3,3,3,256,256]{5,4,3,2,1,0:T(8,128)}) %all-gather.2.cloned.1.call-update) | async-done | bytes 56623120 | tf_op jit(solution)/shard_map/all_gather | solution.py:74
  1169.3 21.5 %reduce_sum.9 = f32[3,3,3,256,256]{4,3,2,1,0:T(8,128)} reduce(f32[8,3,3,3,256,256]{5,4,3,2,1,0:T(8,128)} %all-gather.2.cloned.1.call-done, f32[]{:T(128)} %constant.33.clone.1), dimensions={0}, to_apply=%region_2.3 | reduce | flops 12386304 | bytes 63700996 | tf_op jit(solution)/shard_map/reduce_sum | solution.py:75
  1190.7 8.1 copy.62
  1198.8 6.5 broadcast_multiply_fusion
  1205.4 8.0 copy.61
  (148 shorter events, 39.4 us)
Async XLA Ops:
  8.0 89.4 %reduce-scatter.5.cloned.1.call-start = ((), (), s32[]{:S(2)}) async-start(), calls=%async_computation.3 | async-start | bytes 786432 | tf_op jit(solution)/shard_map/reduce_scatter | solution.py:70
  15.4 30.3 %collective-permute-start.1 = (bf16[1,256,512]{2,1,0:T(8,128)(2,1)S(1)}, bf16[1,256,512]{2,1,0:T(8,128)(2,1)}, u32[]{:S(2)}, u32[]{:S(2)}) collective-permute-start(bf16[1,256,512]{2,1,0:T(8,128)(2,1)S(1)} %all_gather.9), channel_id=1, source_target_pairs={{4,0},{8,4},{12,8},{16,12},{20,16},{24,20},{28,24},{5,1},{9,5},{13... | collective-permute-start | bytes 786440 | tf_op jit(solution)/shard_map/ppermute | solution.py:17
  16.7 29.0 %collective-permute-start = (bf16[1,256,512]{2,1,0:T(8,128)(2,1)S(1)}, bf16[1,256,512]{2,1,0:T(8,128)(2,1)}, u32[]{:S(2)}, u32[]{:S(2)}) collective-permute-start(bf16[1,256,512]{2,1,0:T(8,128)(2,1)S(1)} %all_gather.9), channel_id=1, source_target_pairs={{0,4},{4,8},{8,12},{12,16},{16,20},{20,24},{24,28},{1,5},{5,9},{9,... | collective-permute-start | bytes 786440 | tf_op jit(solution)/shard_map/ppermute | solution.py:16
  24.3 19.3 %collective-permute-start.3 = (bf16[1,256,512]{2,1,0:T(8,128)(2,1)S(1)}, bf16[1,256,512]{2,1,0:T(8,128)(2,1)}, u32[]{:S(2)}, u32[]{:S(2)}) collective-permute-start(bf16[1,256,512]{2,1,0:T(8,128)(2,1)S(1)} %all_gather.10), channel_id=1, source_target_pairs={{4,0},{8,4},{12,8},{16,12},{20,16},{24,20},{28,24},{5,1},{9,5},{13... | collective-permute-start | bytes 786440 | tf_op jit(solution)/shard_map/ppermute | solution.py:17
  25.5 18.0 %collective-permute-start.2 = (bf16[1,256,512]{2,1,0:T(8,128)(2,1)S(1)}, bf16[1,256,512]{2,1,0:T(8,128)(2,1)S(1)}, u32[]{:S(2)}, u32[]{:S(2)}) collective-permute-start(bf16[1,256,512]{2,1,0:T(8,128)(2,1)S(1)} %all_gather.10), channel_id=1, source_target_pairs={{0,4},{4,8},{8,12},{12,16},{16,20},{20,24},{24,28},{1,5},{5,9},{9,... | collective-permute-start | bytes 786440 | tf_op jit(solution)/shard_map/ppermute | solution.py:16
  43.6 2.1 copy-start.18
  49.3 12.1 copy-start.17
  49.3 3.0 copy-start.6
  52.3 1.5 copy-start.5
  53.7 17.5 %copy-start.12 = (bf16[1,256,512]{2,1,0:T(8,128)(2,1)}, bf16[1,256,512]{2,1,0:T(8,128)(2,1)S(1)}, u32[]{:S(2)}) copy-start(bf16[1,256,512]{2,1,0:T(8,128)(2,1)S(1)} %get-tuple-element.89) | copy-start | bytes 786436
  58.2 3.2 copy-start.32
  59.9 1.5 copy-start.33
  59.9 1.5 copy-start.45
  61.1 38.0 %reduce-scatter.3.cloned.1.call-start = ((), (), s32[]{:S(2)}) async-start(), calls=%async_computation.2 | async-start | bytes 786432 | tf_op jit(solution)/shard_map/reduce_scatter | solution.py:69
  69.5 1.3 copy-start.40
  72.0 1.3 copy-start.34
  72.0 1.3 copy-start.35
  72.0 1.3 copy-start.36
  78.9 1.4 copy-start
  78.9 1090.4 %all-gather.2.cloned.1.call-start = ((), (), s32[]{:S(2)}) async-start(), calls=%async_computation.4 | async-start | bytes 63700992 | tf_op jit(solution)/shard_map/all_gather | solution.py:74
  80.2 2.6 copy-start.2
  81.5 2.6 copy-start.1
  82.8 2.6 copy-start.4
  84.1 2.6 copy-start.3
  (29 other events, 30.6 us)
Sparse Core Ops, SparseCore 0:
  61.3 16.0 reduce-scatter.4
  79.7 8.7 reduce-scatter.2
Sparse Core Ops, SparseCore 1:
  97.4 1071.8 all-gather.1
